TPU v7x, 256 devices: a whole 4x4x8 slice. The times are simulated.
256 devices in a mesh: dp: 4 (over x_hi, core), ctx: 64 (over y, z, x_lo).
Axes of the slice: x: 4 (x_hi: 2, x_lo: 2; x = x_hi * 2 + x_lo), y: 4, z: 8, core: 2. Of those that a mesh axis runs over, the one named last changes fastest.
Arguments:
- frames: bfloat16 [4, 12288, 1024], P('dp', 'ctx'), may hold values from -60 to 60
- lengths: int32 [4], P('dp'), may hold values from 6144 to 12288, as said below
- w_qkv: bfloat16 [1024, 1536], replicated, may hold values from -0.9 to 0.9
- w_out: bfloat16 [512, 1024], replicated, may hold values from -0.25 to 0.25
- w_pw1: bfloat16 [1024, 2048], replicated, may hold values from -0.1875 to 0.1875
- conv_taps: float32 [31, 1024], replicated, may hold values from -1 to 1
- w_pw2: bfloat16 [1024, 1024], replicated, may hold values from -0.1875 to 0.1875
Outputs:
- encoded: bfloat16 [4, 12288, 1024], P('dp', 'ctx')
Inputs may be any that keep to these rules, and one draw needn't show every extreme that they name: `lengths`: the valid frames of a recording are its first ones; some recording has all 12288 frames valid.
All inputs are finite; a program needn't handle non-finite values.
Results may differ from a plain program's by a relative error of at most 0.011.
Values may be sent and summed in bfloat16 or wider, within the bound.
A program may use at most 256 MiB of HBM per device.

v0:
```python
import jax
import jax.numpy as jnp
from jax import lax
from jax.sharding import PartitionSpec as P

HEADS = 8
epsilon = 1e-05
masked_score = -1e30


def padded_2(cells, sides, width):
    for axis, dim in sides:
        count = lax.axis_size(axis)
        ends = count - 1
        head = lax.slice_in_dim(cells, 0, width, axis=dim)
        tail = lax.slice_in_dim(cells, cells.shape[dim] - width, cells.shape[dim], axis=dim)
        cells = jnp.concatenate(
            [
                lax.ppermute(tail, axis, [(i, (i + 1) % count) for i in range(ends)]),
                cells,
                lax.ppermute(head, axis, [((i + 1) % count, i) for i in range(ends)]),
            ],
            axis=dim,
        )
    return cells


def to_bf16(value):
    return lax.optimization_barrier(value.astype(jnp.bfloat16))


def layer_norm(value):
    center = value - jnp.mean(value, axis=-1, keepdims=True)
    spread = jnp.mean(center * center, axis=-1, keepdims=True)
    return center * lax.rsqrt(spread + epsilon)


def depthwise(padded, conv_taps, count):
    total = jnp.zeros((count, padded.shape[1]), jnp.float32)
    for tap_index in range(conv_taps.shape[0]):
        total = total + conv_taps[tap_index] * padded[tap_index : tap_index + count].astype(
            jnp.float32
        )
    return total


def gate_rows(stream_rows, spots, limit, w_pw1):
    gated = jnp.dot(
        to_bf16(layer_norm(stream_rows.astype(jnp.float32))),
        w_pw1,
        preferred_element_type=jnp.float32,
    )
    half_cols = gated.shape[1] // 2
    result = gated[:, :half_cols] * jax.nn.sigmoid(gated[:, half_cols:])
    return to_bf16(jnp.where((spots < limit)[:, None], result, 0.0))


def attend_block(carry, query_heads, key_piece, value_piece, limit):
    run_max, run_sum, run_acc = carry
    count = key_piece.shape[0]
    head_count = query_heads.shape[1]
    head_size = query_heads.shape[2]
    key_heads = key_piece.reshape(count, head_count, head_size)
    value_heads = value_piece.reshape(count, head_count, head_size)
    scores = jnp.einsum("qhd,khd->hqk", query_heads, key_heads, preferred_element_type=jnp.float32)
    live = jnp.arange(count, dtype=jnp.int32) < limit
    masked = jnp.where(live, scores, masked_score)
    new_max = jnp.maximum(run_max, jnp.max(masked, axis=-1))
    weights = jnp.where(live, jnp.exp(masked - new_max[:, :, None]), 0.0)
    scale_old = jnp.exp(run_max - new_max)
    new_sum = jnp.sum(weights, axis=-1)
    product = jnp.einsum(
        "hqk,khd->qhd", to_bf16(weights), value_heads, preferred_element_type=jnp.float32
    )
    new_acc = run_acc * scale_old.T[:, :, None] + product
    return (new_max, new_sum, new_acc)


def per_device(frames, lengths, w_qkv, w_out, w_pw1, conv_taps, w_pw2):
    stream = frames[0]
    frame_rows = stream.shape[0]
    my_index = lax.axis_index("ctx")
    my_start = my_index * frame_rows
    limit = lengths[0]
    positions = my_start + jnp.arange(frame_rows, dtype=jnp.int32)
    valid = positions < limit
    normed = to_bf16(layer_norm(stream.astype(jnp.float32)))
    projected = jnp.dot(normed, w_qkv, preferred_element_type=jnp.float32)
    inner = w_out.shape[0]
    head_size = inner // HEADS
    queries = to_bf16(projected[:, :inner] * head_size ** (-0.5)).reshape(
        frame_rows, HEADS, head_size
    )
    keys = to_bf16(projected[:, inner : 2 * inner])
    values = to_bf16(projected[:, 2 * inner :])
    initial = (
        jnp.full((HEADS, frame_rows), masked_score, jnp.float32),
        jnp.zeros((HEADS, frame_rows), jnp.float32),
        jnp.zeros((frame_rows, HEADS, head_size), jnp.float32),
    )
    run_max, run_sum, run_acc = attend_block(
        initial,
        queries,
        lax.all_gather(keys, "ctx", axis=0, tiled=True),
        lax.all_gather(values, "ctx", axis=0, tiled=True),
        limit,
    )
    attended = to_bf16(run_acc / run_sum.T[:, :, None]).reshape(frame_rows, inner)
    first = to_bf16(
        stream.astype(jnp.float32) + jnp.dot(attended, w_out, preferred_element_type=jnp.float32)
    )
    half_width = conv_taps.shape[0] // 2
    gated_own = gate_rows(first, positions, limit, w_pw1)
    padded = padded_2(gated_own, (("ctx", 0),), half_width)
    conv = depthwise(padded, conv_taps, frame_rows)
    swished = to_bf16(jax.nn.silu(layer_norm(conv)))
    second = first.astype(jnp.float32) + jnp.dot(swished, w_pw2, preferred_element_type=jnp.float32)
    encoded = jnp.where(valid[:, None], layer_norm(second), 0.0).astype(jnp.bfloat16)
    return encoded[None]


def solution(mesh):
    in_specs = (P("dp", "ctx", None), P("dp"), P(), P(), P(), P(), P())
    out_specs = P("dp", "ctx", None)
    return jax.shard_map(
        per_device, mesh=mesh, in_specs=in_specs, out_specs=out_specs, check_vma=False
    )
```

profile of v0, /device:TPU:2, one launch (start us, length us, event | category | flops | bytes accessed | tf_op | source)
XLA Modules:
  0.0 736.1 jit_solution(17029172689337861144)
XLA Ops:
  6.5 0.0 copy-start
  6.5 0.0 all-gather.3.cloned.1.call-start
  6.5 1.3 convert_reduce_fusion.1
  7.8 1.2 fusion.13
  9.1 1.2 fusion.14
  10.3 0.0 copy-done
  10.3 1.9 fusion.56
  12.2 0.8 fusion.52
  13.0 0.0 all-gather.3.cloned.1.call-update
  13.0 0.0 all-gather.5.cloned.1.call-start
  13.0 0.7 all-gather.5.cloned.1.call-update
  13.7 1.0 fusion.50
  14.8 0.1 copy.11
  15.6 0.5 add_compare_fusion
  16.1 1.8 fusion.54
  18.0 322.8 %all-gather.3.cloned.1.call-done = bf16[12288,512]{1,0:T(8,128)(2,1)} async-done(((bf16[192,512]{1,0:T(8,128)(2,1)}), bf16[12288,512]{1,0:T(8,128)(2,1)}) %all-gather.3.cloned.1.call-update) | async-done | bytes 12582928 | tf_op jit(solution)/shard_map/all_gather | solution.py:104
  340.7 16.6 %copy.12 = bf16[12288,512]{0,1:T(8,128)(2,1)} copy(bf16[12288,512]{1,0:T(8,128)(2,1)} %all-gather.3.cloned.1.call-done) | data formatting | bytes 25165824 | tf_op jit(solution)/shard_map/all_gather | solution.py:104
  357.3 31.0 %select_reduce_fusion = (f32[8,192]{1,0:T(8,128)S(1)}, f32[8,192,12288]{2,1,0:T(8,128)}) fusion(pred[12288]{0:T(1024)(128)(4,1)S(1)} %iota_compare_fusion, bf16[192,8,64]{0,2,1:T(8,128)(2,1)S(1)} %bitcast.79, bf16[12288,8,64]{0,2,1:T(8,128)(2,1)} %bitcast.78), kind=kOutput, calls=%fused_computation.1 | convolution fusion | flops 2453666304 | bytes 88295424 | tf_op jit(solution)/shard_map/qhd,khd->hqk/dot_general | solution.py:65
  388.4 37.7 %fusion = (f32[8,192]{1,0:T(8,128)S(1)}, bf16[8,192,12288]{2,1,0:T(8,128)(2,1)}) fusion(f32[8,192,12288]{2,1,0:T(8,128)} %get-tuple-element.49, f32[8,192]{1,0:T(8,128)S(1)} %get-tuple-element.45, pred[12288]{0:T(1024)(128)(4,1)S(1)} %iota_compare_fusion), kind=kLoop, calls=%fused_computation.2 | loop fusion | flops 94370304 | bytes 113270784 | tf_op jit(solution)/shard_map/reduce_sum | solution.py:71
  426.0 239.9 %all-gather.5.cloned.1.call-done = bf16[12288,512]{1,0:T(8,128)(2,1)} async-done(((bf16[192,512]{1,0:T(8,128)(2,1)}), bf16[12288,512]{1,0:T(8,128)(2,1)}) %all-gather.5.cloned.1.call-update) | async-done | bytes 12582928 | tf_op jit(solution)/shard_map/all_gather | solution.py:105
  666.0 16.5 %copy.13 = bf16[12288,512]{0,1:T(8,128)(2,1)} copy(bf16[12288,512]{1,0:T(8,128)(2,1)} %all-gather.5.cloned.1.call-done) | data formatting | bytes 25165824 | tf_op jit(solution)/shard_map/all_gather | solution.py:105
  682.5 0.0 copy-start.2
  682.5 0.0 copy-start.1
  682.5 21.5 %fusion.5 = bf16[192,8,64]{0,2,1:T(8,128)(2,1)} fusion(bf16[12288,8,64]{0,2,1:T(8,128)(2,1)} %bitcast.77, bf16[8,192,12288]{2,1,0:T(8,128)(2,1)} %get-tuple-element.8, f32[192,8]{0,1:T(8,128)S(1)} %bitcast.81, f32[192,8]{0,1:T(8,128)S(1)} %get-tuple-element.44), kind=kOutput, calls=%fused_computation.38 | convolution fusion | flops 2416214016 | bytes 50540544 | tf_op jit(solution)/shard_map/hqk,khd->qhd/dot_general | solution.py:72
  703.9 0.0 copy-start.3
  703.9 0.0 copy-start.4
  704.0 0.0 copy-done.2
  704.0 1.9 fusion.2
  705.8 0.1 convert_reduce_fusion
  706.0 0.3 fusion.11
  706.2 0.2 fusion.12
  706.5 3.2 fusion.58
  709.7 0.8 fusion.20
  710.5 4.0 collective-permute-start
  714.5 2.1 collective-permute-start.1
  716.6 1.1 fusion.55
  717.7 0.0 collective-permute-done
  717.8 3.4 collective-permute-done.1
  721.2 5.5 fusion.51
  726.8 0.2 multiply_reduce_fusion.1
  727.0 0.4 multiply_convert_fusion
  727.4 0.0 copy-done.3
  727.4 0.7 fusion.57
  728.1 0.2 multiply_reduce_fusion
  728.3 0.0 copy-done.4
  728.3 0.9 fusion.21
  729.3 0.0 copy-done.1
  (11 shorter events, 0.1 us)
Async XLA Ops:
  6.5 3.8 copy-start
  6.5 334.2 %all-gather.3.cloned.1.call-start = ((), (), s32[]{:S(2)}) async-start(), calls=%async_computation | async-start | bytes 12779520 | tf_op jit(solution)/shard_map/all_gather | solution.py:104
  13.0 653.0 %all-gather.5.cloned.1.call-start = ((), (), s32[]{:S(2)}) async-start(), calls=%async_computation.1 | async-start | bytes 12779520 | tf_op jit(solution)/shard_map/all_gather | solution.py:105
  682.5 21.5 %copy-start.2 = (bf16[1,192,1024]{2,1,0:T(8,128)(2,1)S(1)}, bf16[1,192,1024]{2,1,0:T(8,128)(2,1)}, u32[]{:S(2)}) copy-start(bf16[1,192,1024]{2,1,0:T(8,128)(2,1)} %param.7) | copy-start | bytes 1179652
  682.5 46.8 %copy-start.1 = (bf16[1024,1536]{1,0:T(8,128)(2,1)S(1)}, bf16[1024,1536]{1,0:T(8,128)(2,1)}, u32[]{:S(2)}) copy-start(bf16[1024,1536]{1,0:T(8,128)(2,1)} %param.9) | copy-start | bytes 9437188
  703.9 23.4 %copy-start.3 = (bf16[1024,1024]{1,0:T(8,128)(2,1)S(1)}, bf16[1024,1024]{1,0:T(8,128)(2,1)}, u32[]{:S(2)}) copy-start(bf16[1024,1024]{1,0:T(8,128)(2,1)} %param.13) | copy-start | bytes 6291460
  703.9 24.4 %copy-start.4 = (pred[192]{0:T(512)(128)(4,1)S(1)}, pred[192]{0:T(512)(128)(4,1)}, u32[]{:S(2)}) copy-start(pred[192]{0:T(512)(128)(4,1)} %add_compare_fusion) | copy-start | bytes 580
  710.5 7.2 collective-permute-start
  714.5 6.7 collective-permute-start.1
Sparse Core Ops, SparseCore 0:
  13.1 327.5 all-gather.2
  342.5 323.4 all-gather.4
where the time goes:
time: 737 us; the launch traced here: 736 us
  waiting for transfers between devices  567 us (77%)
  matrix products  60.1 us (8%)
  other arithmetic  51.8 us (7%)
  local copies, waits for them, and re-layouts  37 us (5%)
  between operations  14.2 us (2%)
    all_gather x1, waiting for transfers between devices, per_device(): lax.all_gather(keys, 'ctx', axis=0, tiled=True)  323 us
    all_gather x1, waiting for transfers between devices, per_device(): lax.all_gather(values, 'ctx', axis=0, tiled=True)  240 us
    reduce_sum x1, other arithmetic, attend_block(): new_sum = jnp.sum(weights, axis=-1)  37.7 us
    dot_general x1, matrix products, attend_block(): jnp.einsum('qhd,khd->hqk', query_heads, key_heads, preferred_element_type...  31 us
    dot_general x1, matrix products, attend_block(): jnp.einsum('hqk,khd->qhd', to_bf16(weights), value_heads, preferred_eleme...  21.5 us
    all_gather x1, local copies, waits for them, and re-layouts, per_device(): lax.all_gather(keys, 'ctx', axis=0, tiled=True)  16.6 us
    all_gather x1, local copies, waits for them, and re-layouts, per_device(): lax.all_gather(values, 'ctx', axis=0, tiled=True)  16.5 us
  transfers between devices with their start and end apart: 4, of which 3 were waited for; matrix products, arithmetic and copies ran while one was open for 12% of the time, Pallas kernels for 0%

commit v1 on v0

--- a/solution.py
+++ b/solution.py
@@ -98,10 +98,19 @@
         jnp.zeros((HEADS, frame_rows), jnp.float32),
         jnp.zeros((frame_rows, HEADS, head_size), jnp.float32),
     )
+    follow_digits = lambda vec, at_axis: jnp.concatenate(
+        lax.all_to_all(
+            jnp.stack([vec for _ in range(lax.psum(1, axis_name="ctx"))], 0),
+            axis_name="ctx",
+            split_axis=0,
+            concat_axis=0,
+        ),
+        at_axis,
+    )
     run_max, run_sum, run_acc = attend_block(
         initial,
         queries,
-        lax.all_gather(keys, "ctx", axis=0, tiled=True),
+        follow_digits(keys, 0),
         lax.all_gather(values, "ctx", axis=0, tiled=True),
         limit,
     )

time: 737 us -> 610 us (0.83)
  waiting for transfers between devices: 567 us -> 383 us
  local copies, waits for them, and re-layouts: 37 us -> 74.3 us
  starting transfers between devices: 6.12 us -> 19.7 us
    all_to_all x0 -> x1, waiting for transfers between devices: none -> 350 us  [per_device(): lax.all_to_all(jnp.stack([vec for _ in range(lax.psum(1, axis_name='ctx')...]
    all_gather x1 -> x0, waiting for transfers between devices: 323 us -> none  [per_device(): lax.all_gather(keys, 'ctx', axis=0, tiled=True)]
    all_gather x1, waiting for transfers between devices: 240 us -> 31.2 us  [per_device(): lax.all_gather(values, 'ctx', axis=0, tiled=True)]
    another operation x0 -> x2, local copies, waits for them, and re-layouts: none -> 30.9 us  [the longest x1 24.8 us: attend_block(): key_heads = key_piece.reshape(count, head_count, head_size)]
    all_to_all x0 -> x1, local copies, waits for them, and re-layouts: none -> 24.3 us  [per_device(): lax.all_to_all(jnp.stack([vec for _ in range(lax.psum(1, axis_name='ctx')...]
    all_gather x1 -> x0, local copies, waits for them, and re-layouts: 16.6 us -> none  [per_device(): lax.all_gather(keys, 'ctx', axis=0, tiled=True)]
    all_to_all x0 -> x1, starting transfers between devices: none -> 13.4 us  [per_device(): lax.all_to_all(jnp.stack([vec for _ in range(lax.psum(1, axis_name='ctx')...]
  transfers between devices with their start and end apart: 4 -> 4, of which waited for: 3 -> 3; matrix products, arithmetic and copies ran while one was open for 12% -> 20% of each run, Pallas kernels for 0% -> 0%
where the time goes in v1:
time: 610 us; the launch traced here: 603 us
  waiting for transfers between devices  383 us (63%)
  local copies, waits for them, and re-layouts  74.3 us (12%)
  matrix products  60 us (10%)
  other arithmetic  51.8 us (8%)
  starting transfers between devices  19.7 us (3%)
  between operations  14.2 us (2%)
    all_to_all x1, waiting for transfers between devices, per_device(): lax.all_to_all(jnp.stack([vec for _ in range(lax.psum(1, axis_name='ctx')...  350 us
    reduce_sum x1, other arithmetic, attend_block(): new_sum = jnp.sum(weights, axis=-1)  37.7 us
    all_gather x1, waiting for transfers between devices, per_device(): lax.all_gather(values, 'ctx', axis=0, tiled=True)  31.2 us
    dot_general x1, matrix products, attend_block(): jnp.einsum('qhd,khd->hqk', query_heads, key_heads, preferred_element_type...  31 us
    another operation x1, local copies, waits for them, and re-layouts, attend_block(): key_heads = key_piece.reshape(count, head_count, head_size)  24.8 us
    all_to_all x1, local copies, waits for them, and re-layouts, per_device(): lax.all_to_all(jnp.stack([vec for _ in range(lax.psum(1, axis_name='ctx')...  24.3 us
    dot_general x1, matrix products, attend_block(): jnp.einsum('hqk,khd->qhd', to_bf16(weights), value_heads, preferred_eleme...  21.5 us
    all_gather x1, local copies, waits for them, and re-layouts, per_device(): lax.all_gather(values, 'ctx', axis=0, tiled=True)  16.5 us
  transfers between devices with their start and end apart: 4, of which 3 were waited for; matrix products, arithmetic and copies ran while one was open for 20% of the time, Pallas kernels for 0%

profile of v1, /device:TPU:2, one launch (start us, length us, event | category | flops | bytes accessed | tf_op | source)
XLA Modules:
  0.0 603.3 jit_solution(12797067942810577139)
XLA Ops:
  6.5 0.0 copy-start
  6.5 1.3 convert_reduce_fusion.1
  7.8 1.2 fusion.13
  9.1 1.2 fusion.14
  10.3 0.0 copy-done
  10.3 1.9 fusion.56
  12.2 0.7 fusion.52
  12.9 6.1 %stack.2 = bf16[64,192,512]{2,1,0:T(8,128)(2,1)} broadcast(bf16[192,512]{1,0:T(8,128)(2,1)S(1)} %get-tuple-element.9), dimensions={1,2} | broadcast | bytes 12779520 | tf_op jit(solution)/shard_map/stack | solution.py:103
  19.0 0.0 copy-start.4
  19.0 13.4 %all-to-all-start = ((bf16[64,192,512]{2,1,0:T(8,128)(2,1)}), bf16[64,192,512]{2,1,0:T(8,128)(2,1)}, u32[]{:S(2)}, u32[]{:S(2)}) async-start(bf16[64,192,512]{2,1,0:T(8,128)(2,1)} %stack.2), calls=%async_computation | async-start | bytes 25165824 | tf_op jit(solution)/shard_map/all_to_all | solution.py:102
  32.4 0.2 all-gather.2.cloned.1.call-start
  32.6 0.5 all-gather.2.cloned.1.call-update
  33.1 1.0 fusion.50
  34.2 0.1 copy.14
  35.0 0.5 add_compare_fusion
  35.5 0.0 copy-done.4
  35.5 0.7 fusion.54
  36.2 350.0 %all-to-all-done = bf16[64,192,512]{2,1,0:T(8,128)(2,1)} async-done(((bf16[64,192,512]{2,1,0:T(8,128)(2,1)}), bf16[64,192,512]{2,1,0:T(8,128)(2,1)}, u32[]{:S(2)}, u32[]{:S(2)}) %all-to-all-start) | async-done | bytes 12582944 | tf_op jit(solution)/shard_map/all_to_all | solution.py:102
  386.2 24.3 %copy.15 = bf16[64,192,512]{1,0,2:T(8,128)(2,1)} copy(bf16[64,192,512]{2,1,0:T(8,128)(2,1)} %all-to-all-done) | data formatting | bytes 25165824 | tf_op jit(solution)/shard_map/all_to_all | solution.py:102
  410.5 24.8 %reshape_reshape.3 = bf16[12288,8,64]{0,2,1:T(8,128)(2,1)} reshape(bf16[64,192,512]{1,0,2:T(8,128)(2,1)} %copy.15) | data formatting | bytes 25165824 | tf_op jit(solution)/shard_map/reshape;reshape | solution.py:63
  435.3 31.0 %select_reduce_fusion = (f32[8,192]{1,0:T(8,128)S(1)}, f32[8,192,12288]{2,1,0:T(8,128)}) fusion(pred[12288]{0:T(1024)(128)(4,1)S(1)} %iota_compare_fusion, bf16[192,8,64]{0,2,1:T(8,128)(2,1)S(1)} %bitcast.79, bf16[12288,8,64]{0,2,1:T(8,128)(2,1)} %reshape_reshape.3), kind=kOutput, calls=%fused_computation.1 | convolution fusion | flops 2453666304 | bytes 88295424 | tf_op jit(solution)/shard_map/qhd,khd->hqk/dot_general | solution.py:65
  466.2 37.7 %fusion = (f32[8,192]{1,0:T(8,128)S(1)}, bf16[8,192,12288]{2,1,0:T(8,128)(2,1)}) fusion(f32[8,192,12288]{2,1,0:T(8,128)} %get-tuple-element.49, f32[8,192]{1,0:T(8,128)S(1)} %get-tuple-element.45, pred[12288]{0:T(1024)(128)(4,1)S(1)} %iota_compare_fusion), kind=kLoop, calls=%fused_computation.2 | loop fusion | flops 94370304 | bytes 113270784 | tf_op jit(solution)/shard_map/reduce_sum | solution.py:71
  503.9 31.2 %all-gather.2.cloned.1.call-done = bf16[12288,512]{1,0:T(8,128)(2,1)} async-done(((bf16[192,512]{1,0:T(8,128)(2,1)}), bf16[12288,512]{1,0:T(8,128)(2,1)}) %all-gather.2.cloned.1.call-update) | async-done | bytes 12582928 | tf_op jit(solution)/shard_map/all_gather | solution.py:114
  535.1 16.5 %copy.16 = bf16[12288,512]{0,1:T(8,128)(2,1)} copy(bf16[12288,512]{1,0:T(8,128)(2,1)} %all-gather.2.cloned.1.call-done) | data formatting | bytes 25165824 | tf_op jit(solution)/shard_map/all_gather | solution.py:114
  551.6 0.0 copy-start.2
  551.6 0.0 copy-start.1
  551.6 21.5 %fusion.5 = bf16[192,8,64]{0,2,1:T(8,128)(2,1)} fusion(bf16[12288,8,64]{0,2,1:T(8,128)(2,1)} %bitcast.78, bf16[8,192,12288]{2,1,0:T(8,128)(2,1)} %get-tuple-element.8, f32[192,8]{0,1:T(8,128)S(1)} %bitcast.81, f32[192,8]{0,1:T(8,128)S(1)} %get-tuple-element.44), kind=kOutput, calls=%fused_computation.38 | convolution fusion | flops 2416214016 | bytes 50540544 | tf_op jit(solution)/shard_map/hqk,khd->qhd/dot_general | solution.py:72
  573.1 0.0 copy-done.2
  573.1 1.9 fusion.2
  575.0 0.1 convert_reduce_fusion
  575.1 0.3 fusion.11
  575.4 0.2 fusion.12
  575.6 3.2 fusion.58
  578.8 0.9 fusion.20
  579.7 1.9 collective-permute-start
  581.6 4.1 collective-permute-start.1
  585.8 1.1 fusion.55
  586.9 0.0 collective-permute-done
  586.9 1.4 collective-permute-done.1
  588.4 5.5 fusion.51
  593.9 0.2 multiply_reduce_fusion.1
  594.1 0.4 multiply_convert_fusion
  594.5 0.0 copy-done.3
  594.5 0.7 fusion.57
  595.2 0.2 multiply_reduce_fusion
  595.5 0.0 copy-done.5
  595.5 0.9 fusion.21
  596.4 0.0 copy-done.1
  (13 shorter events, 0.1 us)
Async XLA Ops:
  6.5 3.8 copy-start
  19.0 16.6 %copy-start.4 = (f32[31,1024]{1,0:T(8,128)S(1)}, f32[31,1024]{1,0:T(8,128)}, u32[]{:S(2)}) copy-start(f32[31,1024]{1,0:T(8,128)} %param.12) | copy-start | bytes 380932
  19.0 367.2 %all-to-all-start = ((bf16[64,192,512]{2,1,0:T(8,128)(2,1)}), bf16[64,192,512]{2,1,0:T(8,128)(2,1)}, u32[]{:S(2)}, u32[]{:S(2)}) async-start(bf16[64,192,512]{2,1,0:T(8,128)(2,1)} %stack.2), calls=%async_computation | async-start | bytes 25165824 | tf_op jit(solution)/shard_map/all_to_all | solution.py:102
  32.4 502.7 %all-gather.2.cloned.1.call-start = ((), (), s32[]{:S(2)}) async-start(), calls=%async_computation.1 | async-start | bytes 12779520 | tf_op jit(solution)/shard_map/all_gather | solution.py:114
  551.6 21.5 %copy-start.2 = (bf16[1,192,1024]{2,1,0:T(8,128)(2,1)S(1)}, bf16[1,192,1024]{2,1,0:T(8,128)(2,1)}, u32[]{:S(2)}) copy-start(bf16[1,192,1024]{2,1,0:T(8,128)(2,1)} %param.7) | copy-start | bytes 1179652
  551.6 44.8 %copy-start.1 = (bf16[1024,1536]{1,0:T(8,128)(2,1)S(1)}, bf16[1024,1536]{1,0:T(8,128)(2,1)}, u32[]{:S(2)}) copy-start(bf16[1024,1536]{1,0:T(8,128)(2,1)} %param.9) | copy-start | bytes 9437188
  573.1 21.4 %copy-start.3 = (bf16[1024,1024]{1,0:T(8,128)(2,1)S(1)}, bf16[1024,1024]{1,0:T(8,128)(2,1)}, u32[]{:S(2)}) copy-start(bf16[1024,1024]{1,0:T(8,128)(2,1)} %param.13) | copy-start | bytes 6291460
  573.1 22.4 %copy-start.5 = (pred[192]{0:T(512)(128)(4,1)S(1)}, pred[192]{0:T(512)(128)(4,1)}, u32[]{:S(2)}) copy-start(pred[192]{0:T(512)(128)(4,1)} %add_compare_fusion) | copy-start | bytes 580
  579.7 7.2 %collective-permute-start = (bf16[15,1024]{1,0:T(8,128)(2,1)S(1)}, bf16[15,1024]{1,0:T(8,128)(2,1)S(1)}, u32[]{:S(2)}, u32[]{:S(2)}) collective-permute-start(bf16[15,1024]{1,0:T(8,128)(2,1)S(1)} %get-tuple-element.11), channel_id=1, source_target_pairs={{0,1},{1,2},{2,3},{3,4},{4,5},{5,6},{6,7},{7,8},{8,9},{9,10},{10,1... | collective-permute-start | bytes 92168 | tf_op jit(solution)/shard_map/ppermute | solution.py:19
  581.6 6.7 %collective-permute-start.1 = (bf16[15,1024]{1,0:T(8,128)(2,1)S(1)}, bf16[15,1024]{1,0:T(8,128)(2,1)S(1)}, u32[]{:S(2)}, u32[]{:S(2)}) collective-permute-start(bf16[15,1024]{1,0:T(8,128)(2,1)S(1)} %get-tuple-element.12), channel_id=1, source_target_pairs={{1,0},{2,1},{3,2},{4,3},{5,4},{6,5},{7,6},{8,7},{9,8},{10,9},{11,1... | collective-permute-start | bytes 92168 | tf_op jit(solution)/shard_map/ppermute | solution.py:21
Sparse Core Ops, SparseCore 0:
  35.0 500.0 all-gather.1
